TPU v7x, 512 devices: a whole 4x4x16 slice. The times are simulated.
512 devices in a mesh: row: 32 (over z, x_hi), col: 16 (over x_lo, y, core).
Axes of the slice: x: 4 (x_hi: 2, x_lo: 2; x = x_hi * 2 + x_lo), y: 4, z: 16, core: 2. Of those that a mesh axis runs over, the one named last changes fastest.
Arguments:
- inverse_set: float32 [1, 32, 128, 2, 16, 128], P(None, 'row', None, None, 'col'), may hold values from -6 to 6
- presence: int32 [1, 32, 2, 16], P(None, 'row', None, 'col'), may hold values 0 or 1
- factor: float32 [1, 32, 128, 512], P(None, 'row'), may hold values from -0.09375 to 0.09375
- dinv: float32 [512, 512], P('row', 'col'), may hold values from -6 to 6
Outputs:
- off_diag: float32 [1, 32, 128, 512], P(None, 'row', 'col')
- diag_block: float32 [512, 512], P('row', 'col')
All inputs are finite; a program needn't handle non-finite values. No bound on the sum of `presence` on one device may be relied on, other than what follows from the above.
Results may differ from a plain program's by a relative error of at most 0.00007.
Values sent between devices are 32-bit elements; how exact they have to be, the bound alone decides.
A program may use at most 64 MiB of HBM per device.

v0:
```python
import jax
import jax.numpy as jnp
from jax import lax
from jax.sharding import PartitionSpec as P


def spread(value, axis, root):
    mine = lax.axis_index(axis) == root
    return lax.psum(jnp.where(mine, value, jnp.zeros_like(value)), axis)


def local(inverse_set, presence, factor, dinv):
    groups_row = lax.axis_size("row")
    groups_col = lax.axis_size("col")
    group_ratio = groups_row // groups_col
    col_index = lax.axis_index("col")
    block_order = factor.shape[2]
    width = factor.shape[3]
    block_cols = inverse_set.shape[3]
    own_rows = factor[:, 0]
    masked = (
        inverse_set[:, 0, :, :, 0, :] * presence[:, 0, :, 0].astype(jnp.float32)[:, None, :, None]
    )
    pieces = []
    for level in range(group_ratio):
        pieces.append(spread(own_rows, "row", level * groups_col + col_index))
    columns = jnp.stack(pieces, axis=1).reshape(block_cols, block_order, width)
    partial_value = jnp.einsum("axbz,bzy->axy", masked, columns, precision=lax.Precision.HIGHEST)
    update = lax.psum_scatter(partial_value, "col", scatter_dimension=1, tiled=True)
    share = block_order // groups_col
    rows_mine = lax.dynamic_slice_in_dim(own_rows, col_index * share, share, 1)
    diag_part = jnp.einsum("axy,axw->yw", rows_mine, update, precision=lax.Precision.HIGHEST)
    diag_half = lax.psum_scatter(diag_part, "col", scatter_dimension=1, tiled=True)
    diag_sum = lax.psum_scatter(diag_half, "row", scatter_dimension=0, tiled=True)
    off_diag = (-update)[:, None, :, :]
    diag_block = dinv + diag_sum
    return (off_diag, diag_block)


def solution(mesh):
    in_specs = (
        P(None, "row", None, None, "col", None),
        P(None, "row", None, "col"),
        P(None, "row", None, None),
        P("row", "col"),
    )
    out_specs = (P(None, "row", "col", None), P("row", "col"))
    return jax.shard_map(local, mesh=mesh, in_specs=in_specs, out_specs=out_specs, check_vma=False)
```

profile of v0, /device:TPU:8, one launch (start us, length us, event | category | flops | bytes accessed | tf_op | source)
XLA Modules:
  0.0 1117.5 jit_solution(4744221916118201594)
XLA Ops:
  7.2 0.0 all-reduce.3.cloned.1.call-start
  7.2 1.8 broadcast_select_fusion.1
  9.0 0.0 all-reduce.3.cloned.1.call-update
  9.1 0.0 reduce-scatter.6.cloned.1.call-start
  9.1 0.6 copy-done.3
  9.7 0.3 copy-done
  9.9 0.2 broadcast_multiply_fusion
  10.1 316.0 %all-reduce.3.cloned.1.call-done = (f32[1,1,128,512]{3,2,1,0:T(8,128)}, f32[1,1,128,512]{3,2,1,0:T(8,128)}) async-done(((f32[1,1,128,512]{3,2,1,0:T(8,128)}, f32[1,1,128,512]{3,2,1,0:T(8,128)}), (f32[1,1,128,512]{3,2,1,0:T(8,128)}, f32[1,1,128,512]{3,2,1,0:T(8,128)})) %all-reduce.3.cloned.1.call-update) | async-done | bytes 524304 | tf_op jit(solution)/shard_map/psum | solution.py:9
  326.1 2.1 convolution_bitcast_fusion
  328.3 0.0 reduce-scatter.6.cloned.1.call-update
  328.3 0.0 reduce-scatter.8.cloned.1.call-start
  328.4 61.3 %reduce-scatter.6.cloned.1.call-done = f32[1,8,512]{2,1,0:T(8,128)} async-done(((f32[1,128,512]{2,1,0:T(8,128)}), f32[1,8,512]{2,1,0:T(8,128)}) %reduce-scatter.6.cloned.1.call-update) | async-done | bytes 16400 | tf_op jit(solution)/shard_map/reduce_scatter | solution.py:29
  389.6 2.7 fusion.3
  392.4 0.0 reduce-scatter.8.cloned.1.call-update
  392.4 0.0 reduce-scatter.10.cloned.1.call-start
  392.4 0.6 copy-done.2
  393.1 0.1 copy.10
  393.1 67.8 %reduce-scatter.8.cloned.1.call-done = f32[512,32]{0,1:T(8,128)} async-done(((f32[512,512]{0,1:T(8,128)}), f32[512,32]{0,1:T(8,128)}) %reduce-scatter.8.cloned.1.call-update) | async-done | bytes 65552 | tf_op jit(solution)/shard_map/reduce_scatter | solution.py:33
  460.9 1.7 copy.12
  462.6 0.7 copy-done.1
  463.3 0.6 negate_bitcast_fusion
  463.9 645.6 %reduce-scatter.10.cloned.1.call-done = f32[16,32]{1,0:T(8,128)} async-done(((f32[512,32]{1,0:T(8,128)}), f32[16,32]{1,0:T(8,128)}) %reduce-scatter.10.cloned.1.call-update) | async-done | bytes 2064
  1109.5 0.8 copy.13
  1110.3 0.7 copy.11
  (7 shorter events, 0.0 us)
Async XLA Ops:
  7.2 319.0 %all-reduce.3.cloned.1.call-start = ((), (), s32[]{:S(2)}) async-start(), calls=%async_computation.6 | async-start | bytes 1048576 | tf_op jit(solution)/shard_map/psum | solution.py:9
  9.0 0.7 copy-start.3
  9.0 0.9 copy-start
  9.1 380.6 %reduce-scatter.6.cloned.1.call-start = ((), (), s32[]{:S(2)}) async-start(), calls=%async_computation.3 | async-start | bytes 278528 | tf_op jit(solution)/shard_map/reduce_scatter | solution.py:29
  328.3 132.6 %reduce-scatter.8.cloned.1.call-start = ((), (), s32[]{:S(2)}) async-start(), calls=%async_computation.4 | async-start | bytes 1114112 | tf_op jit(solution)/shard_map/reduce_scatter | solution.py:33
  392.4 0.7 copy-start.2
  392.4 717.1 %reduce-scatter.10.cloned.1.call-start = ((), (), s32[]{:S(2)}) async-start(), calls=%async_computation.5 | async-start | bytes 270336
  462.6 0.7 copy-start.1
Sparse Core Ops, SparseCore 0:
  10.9 315.1 all-reduce.2
  328.9 60.6 reduce-scatter.5
  392.5 68.3 reduce-scatter.7
  465.2 644.2 reduce-scatter.9
where the time goes:
time: 1120 us
  waiting for transfers between devices  1090 us (97%)
  between operations  13.8 us (1%)
    unnamed x5, waiting for transfers between devices  646 us
    psum x1, waiting for transfers between devices, spread(): return lax.psum(jnp.where(mine, value, jnp.zeros_like(value)), axis)  316 us
    reduce_scatter x1, waiting for transfers between devices, local(): lax.psum_scatter(diag_part, 'col', scatter_dimension=1, tiled=True)  67.8 us
    reduce_scatter x1, waiting for transfers between devices, local(): lax.psum_scatter(partial_value, 'col', scatter_dimension=1, tiled=True)  61.3 us
  transfers between devices with their start and end apart: 4, of which 4 were waited for; matrix products, arithmetic and copies ran while one was open for 0% of the time, Pallas kernels for 0%

commit v1 on v0

--- a/solution.py
+++ b/solution.py
@@ -6,7 +6,7 @@
 
 def spread(value, axis, root):
     mine = lax.axis_index(axis) == root
-    return lax.psum(jnp.where(mine, value, jnp.zeros_like(value)), axis)
+    return jnp.sum(lax.all_gather(jnp.where(mine, value, jnp.zeros_like(value)), axis), axis=0)
 
 
 def local(inverse_set, presence, factor, dinv):

time: 1120 us -> 1190 us (1.062)
  the two profiles are of different devices: /device:TPU:8 before, /device:TPU:16 now
where the time goes in v1:
time: 1190 us
  waiting for transfers between devices  1160 us (97%)
  between operations  13.8 us (1%)
  other arithmetic  13.4 us (1%)
    unnamed x6, waiting for transfers between devices  649 us
    all_gather x2, waiting for transfers between devices, spread(): lax.all_gather(jnp.where(mine, value, jnp.zeros_like(value)), axis)  381 us
    reduce_scatter x1, waiting for transfers between devices, local(): lax.psum_scatter(diag_part, 'col', scatter_dimension=1, tiled=True)  68.7 us
    reduce_scatter x1, waiting for transfers between devices, local(): lax.psum_scatter(partial_value, 'col', scatter_dimension=1, tiled=True)  56.7 us
  transfers between devices with their start and end apart: 5, of which 5 were waited for; matrix products, arithmetic and copies ran while one was open for 1% of the time, Pallas kernels for 0%

profile of v1, /device:TPU:16, one launch (start us, length us, event | category | flops | bytes accessed | tf_op | source)
XLA Modules:
  0.0 1189.8 jit_solution(12443042006656812910)
XLA Ops:
  7.2 0.0 all-gather.3.cloned.1.call-start
  7.2 1.8 broadcast_select_fusion.1
  9.0 0.0 all-gather.3.cloned.1.call-update
  9.1 0.0 all-gather.5.cloned.1.call-start
  9.1 0.7 all-gather.5.cloned.1.call-update
  9.8 0.0 reduce-scatter.6.cloned.1.call-start
  9.8 0.7 convert_bitcast_fusion
  10.5 1.1 broadcast_multiply_fusion
  11.6 195.6 %all-gather.3.cloned.1.call-done = f32[32,1,128,512]{3,2,1,0:T(8,128)} async-done(((f32[1,1,128,512]{3,2,1,0:T(8,128)}), f32[32,1,128,512]{3,2,1,0:T(8,128)}) %all-gather.3.cloned.1.call-update) | async-done | bytes 8388624 | tf_op jit(solution)/shard_map/all_gather | solution.py:9
  207.2 4.3 reduce_sum.18
  211.5 185.5 %all-gather.5.cloned.1.call-done = f32[32,1,128,512]{3,2,1,0:T(8,128)} async-done(((f32[1,1,128,512]{3,2,1,0:T(8,128)}), f32[32,1,128,512]{3,2,1,0:T(8,128)}) %all-gather.5.cloned.1.call-update) | async-done | bytes 8388624 | tf_op jit(solution)/shard_map/all_gather | solution.py:9
  397.0 4.3 reduce_sum.19
  401.2 1.1 convolution_bitcast_fusion
  402.4 0.0 reduce-scatter.8.cloned.1.call-start
  402.4 56.7 %reduce-scatter.6.cloned.1.call-done = f32[1,8,512]{2,1,0:T(8,128)} async-done(((f32[1,128,512]{2,1,0:T(8,128)}), f32[1,8,512]{2,1,0:T(8,128)}) %reduce-scatter.6.cloned.1.call-update) | async-done | bytes 16400 | tf_op jit(solution)/shard_map/reduce_scatter | solution.py:29
  459.1 2.7 fusion.3
  461.9 0.0 reduce-scatter.10.cloned.1.call-start
  461.9 0.1 copy.10
  462.0 68.7 %reduce-scatter.8.cloned.1.call-done = f32[512,32]{0,1:T(8,128)} async-done(((f32[512,512]{0,1:T(8,128)}), f32[512,32]{0,1:T(8,128)}) %reduce-scatter.8.cloned.1.call-update) | async-done | bytes 65552 | tf_op jit(solution)/shard_map/reduce_scatter | solution.py:33
  530.6 1.7 copy.12
  532.3 1.3 negate_bitcast_fusion
  533.7 648.2 %reduce-scatter.10.cloned.1.call-done = f32[16,32]{1,0:T(8,128)} async-done(((f32[512,32]{1,0:T(8,128)}), f32[16,32]{1,0:T(8,128)}) %reduce-scatter.10.cloned.1.call-update) | async-done | bytes 2064
  1181.8 0.8 copy.13
  1182.6 0.7 copy.11
  (6 shorter events, 0.1 us)
Async XLA Ops:
  7.2 200.1 %all-gather.3.cloned.1.call-start = ((), (), s32[]{:S(2)}) async-start(), calls=%async_computation.3 | async-start | bytes 8650752 | tf_op jit(solution)/shard_map/all_gather | solution.py:9
  9.1 387.9 %all-gather.5.cloned.1.call-start = ((), (), s32[]{:S(2)}) async-start(), calls=%async_computation.4 | async-start | bytes 8650752 | tf_op jit(solution)/shard_map/all_gather | solution.py:9
  9.8 449.3 %reduce-scatter.6.cloned.1.call-start = ((), (), s32[]{:S(2)}) async-start(), calls=%async_computation.5 | async-start | bytes 278528 | tf_op jit(solution)/shard_map/reduce_scatter | solution.py:29
  11.6 450.3 %copy-start = (f32[16,32]{1,0:T(8,128)S(1)}, f32[16,32]{1,0:T(8,128)}, u32[]{:S(2)}) copy-start(f32[16,32]{1,0:T(8,128)} %param.7) | copy-start | bytes 6148
  402.4 128.3 %reduce-scatter.8.cloned.1.call-start = ((), (), s32[]{:S(2)}) async-start(), calls=%async_computation.6 | async-start | bytes 1114112 | tf_op jit(solution)/shard_map/reduce_scatter | solution.py:33
  461.9 720.0 %reduce-scatter.10.cloned.1.call-start = ((), (), s32[]{:S(2)}) async-start(), calls=%async_computation.7 | async-start | bytes 270336
Sparse Core Ops, SparseCore 0:
  11.1 196.1 all-gather.2
  210.3 186.5 all-gather.4
  402.5 56.5 reduce-scatter.5
  462.0 68.6 reduce-scatter.7
  534.9 646.9 reduce-scatter.9
